TPU v7x, 32 devices: a whole 2x2x4 slice. The times are simulated.
32 devices in a mesh: pb: 8 (over y, x, core), pa: 4 (over z).
Axes of the slice: x: 2, y: 2, z: 4, core: 2. Of those that a mesh axis runs over, the one named last changes fastest.
Arguments:
- queries: bfloat16 [2048, 128], P('pb'), may hold values from -10.5 to 10.5, as said below
- encoder_outputs: bfloat16 [8, 64, 128, 1024], P('pb', 'pa'), may hold values from -6 to 6
- proj_weight: bfloat16 [1024, 128], replicated, may hold values from -0.1875 to 0.1875
- bm25_rank: int32 [64, 4, 64], P('pb', 'pa'), may hold values from 0 to 199
- dense_rank: int32 [64, 4, 64], P('pb', 'pa'), may hold values from 0 to 199
- custodian_document_index: int32 [8, 64], P('pb', 'pa'), may hold values from -1 to 31, as said below
Outputs:
- query_grad: float32 [2048, 128], P(('pb', 'pa'))
- encoder_output_derivative: bfloat16 [8, 64, 128, 1024], P('pb', 'pa')
Inputs may be any that keep to these rules, and one draw needn't show every extreme that they name: `queries`: A custom draw: each entry lies between the bounds; rows may differ in scale. `custodian_document_index`: within each row b every number n from 0 to 31 appears exactly once and stands for passage (n // 8, b * 8 + n % 8); all other entries are -1. The owner of columns o * 16 to o * 16 + 15 is index o of pa; an owner holds 0, 8 or 16 passages, and at most 4 with the same n // 8. Some owner is full and some owner holds exactly 4 passages with the same n // 8 in every row.
All inputs are finite; a program needn't handle non-finite values.
Results may differ from a plain program's by a relative error of at most 0.025.
The roundings to bfloat16 on the way count: a program that leaves them out, or rounds other values in their place, can miss the bound.
Values may be sent and summed in bfloat16 or wider, within the bound.
A program may use at most 64 MiB of HBM per device.

v0:
```python
import functools
import math

import jax
import jax.numpy as jnp
from jax import lax
from jax.experimental import pallas as pl
from jax.experimental.pallas import tpu as pltpu
from jax.sharding import PartitionSpec as P

DEPTH = 100

tau = 0.05
inv_temp = 20.0
rrf_offset = 60.0
norm_eps = 1e-06

MESH = pl.DeviceIdType.MESH
F32 = jnp.float32
BF16 = jnp.bfloat16


def joined_target(bm25_rank, dense_rank):
    first = jnp.where(bm25_rank < DEPTH, rrf_offset / (rrf_offset + bm25_rank.astype(F32)), 0.0)
    second = jnp.where(dense_rank < DEPTH, rrf_offset / (rrf_offset + dense_rank.astype(F32)), 0.0)
    return first + second


def xor(a, b, size):
    total = 0
    bit = 1
    while bit < size:
        total = total + ((a // bit + b // bit) % 2) * bit
        bit *= 2
    return total


def three_parts(x):
    first = x.astype(BF16)
    rest = x - first.astype(F32)
    second = rest.astype(BF16)
    third = (rest - second.astype(F32)).astype(BF16)
    return first, second, third


def nt_dot(a, b):
    return lax.dot_general(a, b, (((1,), (1,)), ((), ())), preferred_element_type=F32)


def nn_dot(a, b):
    return jnp.dot(a, b, preferred_element_type=F32)


def step_kernel(
    n_pb, n_pa, slots, length, pd, tokens,
    q_ref, x_ref, w_ref, bm_ref, de_ref, idx_ref,
    pg_ref, qg_ref,
    x_buf, w_buf, bm_buf, de_buf, idx_buf,
    unit, scale, emb, emb_t, prob, coef, lse_buf, inv_buf,
    q_buf, t_buf, t_own, t_exp, dq_keep, dq_out, dq_part, dq_in, sum_out, sum_in,
    x_sem, i_sem, q_send, q_recv, t_send, t_recv, u_send, u_recv, p_send, p_recv, d_send, d_recv, s_send, s_recv,
):
    b = lax.axis_index("pb")
    o = lax.axis_index("pa")
    rows = q_ref.shape[0]
    q_count, m_all = bm_ref.shape
    piece = rows // n_pa
    chunk = 4 if slots % 4 == 0 else 1

    def x_copy(k):
        part = pl.ds(k * length, length)
        return pltpu.make_async_copy(x_ref.at[part], x_buf.at[part], x_sem.at[k])

    def q_copy(d):
        return pltpu.make_async_remote_copy(
            q_buf.at[d - 1 if d % 2 else 0], q_buf.at[d], q_send.at[d], q_recv.at[d],
            device_id={"pb": xor(b, 1 if d % 2 else d, n_pb)}, device_id_type=MESH)

    def t_copy(d):
        return pltpu.make_async_remote_copy(
            t_buf.at[0], t_buf.at[d], t_send.at[d], t_recv.at[d],
            device_id={"pb": xor(b, d, n_pb)}, device_id_type=MESH)

    def u_copy(e):
        return pltpu.make_async_remote_copy(
            t_own.at[0], t_own.at[e], u_send.at[e], u_recv.at[e],
            device_id={"pa": (o + e) % n_pa}, device_id_type=MESH)

    def p_copy(d):
        h = d // 2
        return pltpu.make_async_remote_copy(
            dq_out.at[d], dq_part.at[h], p_send.at[h], p_recv.at[h],
            device_id={"pb": xor(b, 1, n_pb)}, device_id_type=MESH)

    def d_copy(d):
        h = d // 2
        return pltpu.make_async_remote_copy(
            dq_out.at[d], dq_in.at[h], d_send.at[h], d_recv.at[h],
            device_id={"pb": xor(b, d, n_pb)}, device_id_type=MESH)

    def s_copy(e):
        to = (o + e) % n_pa
        return pltpu.make_async_remote_copy(
            sum_out.at[pl.ds(pl.multiple_of(to * piece, piece), piece)],
            sum_in.at[e], s_send.at[e], s_recv.at[e],
            device_id={"pa": to}, device_id_type=MESH)

    barrier = pltpu.get_barrier_semaphore()
    for d in range(1, n_pb):
        pl.semaphore_signal(barrier, inc=1, device_id={"pb": xor(b, d, n_pb)}, device_id_type=MESH)
    for e in range(1, n_pa):
        pl.semaphore_signal(barrier, inc=1, device_id={"pa": (o + e) % n_pa}, device_id_type=MESH)

    small = [
        pltpu.make_async_copy(src, dst, i_sem.at[n])
        for n, (src, dst) in enumerate((
            (w_ref, w_buf), (q_ref, q_buf.at[0]), (bm_ref, bm_buf), (de_ref, de_buf),
            (idx_ref, idx_buf)))
    ]
    small[2].start()
    small[3].start()
    small[0].start()
    for k in range(slots):
        x_copy(k).start()
        if k == chunk - 1:
            small[1].start()
            small[4].start()

    def project(c):
        part = pl.ds(c * chunk * length, chunk * length)
        for k in range(c * chunk, (c + 1) * chunk):
            x_copy(k).wait()
        projected = nn_dot(x_buf[part, :], w_buf[...])
        scaling = lax.rsqrt(jnp.sum(projected * projected, axis=1, keepdims=True) + norm_eps)
        unit_c = projected * scaling
        unit[part, :] = unit_c
        scale[part, :] = scaling
        emb[part, :] = unit_c.astype(BF16)
        emb_t[:, part] = jnp.transpose(unit_c).astype(BF16)

    def send_first():
        pl.semaphore_wait(barrier, n_pb + n_pa - 2)
        for d in range(1, n_pb):
            t_copy(d).start()
        q_copy(1).start()
        for d in range(2, n_pb, 2):
            q_copy(d).start()

    def send_second():
        for d in range(1, n_pb):
            t_copy(d).wait_recv()
        row = lax.broadcasted_iota(jnp.int32, (pd, m_all), 0)
        at = lax.broadcasted_iota(jnp.int32, (pd, m_all), 1)
        pick = jnp.where(at == row + b * pd, 1.0, 0.0).astype(BF16)
        table = t_buf[:, :, 0:m_all].reshape(n_pb * q_count, m_all)
        first, second, third = three_parts(table)
        t_own[0, :, 0:n_pb * q_count] = nt_dot(pick, first) + nt_dot(pick, second) + nt_dot(pick, third)
        for e in range(1, n_pa):
            u_copy(e).start()

    small[2].wait()
    small[3].wait()
    t_buf[0, :, 0:m_all] = joined_target(bm_buf[...], de_buf[...])
    small[0].wait()
    chunks = slots // chunk
    first_at = max(chunks - 2, 0)
    for c in range(chunks):
        project(c)
        if c == first_at:
            small[1].wait()
            small[4].wait()
            send_first()

    same_query = jnp.where(
        lax.broadcasted_iota(jnp.int32, (rows, rows), 0) // tokens
        == lax.broadcasted_iota(jnp.int32, (rows, rows), 1) // tokens, 1.0, 0.0).astype(BF16)
    across = jnp.broadcast_to(idx_buf[...], (slots, slots))
    on_diagonal = lax.broadcasted_iota(jnp.int32, (slots, slots), 0) == lax.broadcasted_iota(
        jnp.int32, (slots, slots), 1)
    held = jnp.sum(jnp.where(on_diagonal, across, 0).astype(F32), axis=1, keepdims=True)
    held = held.astype(jnp.int32)
    filled = held >= 0

    def score_slot(k, q_rows, prob, lse, inv):
        part = pl.ds(k * length, length)
        raw = nt_dot(emb[part, :], q_rows)
        largest = jnp.max(raw, axis=0, keepdims=True)
        power = jnp.exp2((raw - largest) * (inv_temp * math.log2(math.e)))
        total = jnp.sum(power, axis=0, keepdims=True)
        prob[part, :] = power
        lse[pl.ds(k, 1), :] = largest * inv_temp + jnp.log(total)
        inv[pl.ds(k, 1), :] = 1.0 / total

    def factor_of(d, lse, inv):
        first, second, third = three_parts(lse[...])
        score = nn_dot(first, same_query) + nn_dot(second, same_query) + nn_dot(third, same_query)
        residual = (score * (tau / tokens) - t_exp[d]).astype(BF16).astype(F32)
        return jnp.where(filled, residual * (1.0 / tokens) * inv[...], 0.0)

    def spread_targets():
        for e in range(1, n_pa):
            u_copy(e).wait_recv()
        row = lax.broadcasted_iota(jnp.int32, (slots, pd), 1)
        picked = jnp.zeros((slots, n_pb * q_count), F32)
        for e in range(n_pa):
            shard = (o - e + n_pa) % n_pa
            one_hot = jnp.where(held == row + shard * pd, 1.0, 0.0).astype(BF16)
            for part in three_parts(t_own[e, :, 0:n_pb * q_count]):
                picked = picked + nn_dot(one_hot, part)
        picked_parts = jnp.concatenate(
            [p.astype(F32) for p in three_parts(picked)], axis=0).astype(BF16)
        row_at = lax.broadcasted_iota(jnp.int32, (n_pb * q_count, rows), 0)
        lane_at = lax.broadcasted_iota(jnp.int32, (n_pb * q_count, rows), 1)
        for d in range(n_pb):
            spread = jnp.where(row_at == d * q_count + lane_at // tokens, 1.0, 0.0).astype(BF16)
            wide = nn_dot(picked_parts, spread)
            t_exp[d] = wide[0:slots] + wide[slots:2 * slots] + wide[2 * slots:3 * slots]

    grad_order = list(range(2, n_pb)) + [1, 0]
    ring = prob.shape[0] - 2
    lag = ring + 1

    def slot_of(d):
        return d if d < 2 else 2 + (d - 2) % ring

    def scores(d):
        if d > 0:
            q_copy(d).wait_recv()
        if d > 1 and d % 2 == 0:
            q_copy(d + 1).start()
        slot = slot_of(d)
        q_rows = q_buf[d]
        for k in range(slots):
            score_slot(k, q_rows, prob.at[slot], lse_buf.at[slot], inv_buf.at[slot])

    def finish_pair(d):
        p_copy(d + 1).wait_recv()
        dq_out[d] = (dq_keep[d // 2] + dq_part[d // 2].astype(F32)).astype(BF16)
        d_copy(d).start()

    def grads(i):
        d = grad_order[i]
        slot = slot_of(d)
        factor = factor_of(d, lse_buf.at[slot], inv_buf.at[slot])
        lanes = pl.ds(d * rows, rows)
        for k in range(slots):
            part = pl.ds(k * length, length)
            coef[part, lanes] = (prob[slot, part, :] * factor[k:k + 1, :]).astype(BF16)
        dq = nn_dot(emb_t[...], coef[:, lanes])
        if d % 2:
            dq_out[d] = dq.astype(BF16)
            p_copy(d).start()
        else:
            dq_keep[d // 2] = dq
        before = grad_order[i - 1]
        if i > 0 and before % 2 and before > 1:
            finish_pair(before - 1)

    for i in range(n_pb + lag):
        if i < n_pb:
            scores(i)
        if i == 1:
            send_second()
        if i == lag:
            spread_targets()
        if i >= lag:
            grads(i - lag)
    def passage_grad(c):
        part = pl.ds(c * chunk * length, chunk * length)
        q_all = q_buf[...].reshape(n_pb * rows, q_ref.shape[1])
        slot_grad = nn_dot(coef[part, :], q_all).astype(BF16).astype(F32)
        unit_c = unit[part, :]
        inner = jnp.sum(unit_c * slot_grad, axis=1, keepdims=True)
        pg_ref[part, :] = ((slot_grad - unit_c * inner) * scale[part, :]).astype(BF16)

    for c in range(chunks // 4):
        passage_grad(c)
    p_copy(1).wait_recv()
    total = dq_keep[0] + dq_part[0].astype(F32)
    for d in range(n_pb - 2, 0, -2):
        d_copy(d).wait_recv()
        total = total + dq_in[d // 2].astype(F32)
    sum_out[...] = jnp.transpose(total).astype(BF16)
    for e in range(1, n_pa):
        s_copy(e).start()
    for c in range(chunks // 4, chunks):
        passage_grad(c)
    mine = sum_out[pl.ds(pl.multiple_of(o * piece, piece), piece), :].astype(F32)
    for e in range(1, n_pa):
        s_copy(e).wait_recv()
        mine = mine + sum_in[e].astype(F32)
    qg_ref[...] = mine

    for d in range(1, n_pb):
        t_copy(d).wait_send()
        q_copy(d).wait_send()
        if d % 2:
            p_copy(d).wait_send()
        else:
            d_copy(d).wait_send()
    for e in range(1, n_pa):
        u_copy(e).wait_send()
        s_copy(e).wait_send()


def solution(mesh):
    n_pb, n_pa = mesh.shape["pb"], mesh.shape["pa"]

    def on_device(queries, encoder_outputs, proj_weight, bm25_rank, dense_rank, custodian):
        _, slots, length, hidden = encoder_outputs.shape
        dim = proj_weight.shape[1]
        rows = queries.shape[0]
        q_count, _, m_all = bm25_rank.shape
        pd = m_all // n_pb
        tokens = rows // q_count
        all_rows = slots * length
        piece = rows // n_pa
        half = n_pb // 2
        held = 5
        vmem = pl.BlockSpec(memory_space=pltpu.VMEM)
        dma = pltpu.SemaphoreType.DMA
        proj_grad, query_grad = pl.pallas_call(
            functools.partial(step_kernel, n_pb, n_pa, slots, length, pd, tokens),
            out_shape=(
                jax.ShapeDtypeStruct((all_rows, dim), BF16),
                jax.ShapeDtypeStruct((piece, dim), F32),
            ),
            in_specs=[pl.BlockSpec(memory_space=pl.ANY)] * 6,
            out_specs=(vmem, vmem),
            scratch_shapes=[
                pltpu.VMEM((all_rows, hidden), BF16),
                pltpu.VMEM((hidden, dim), BF16),
                pltpu.VMEM((q_count, m_all), jnp.int32),
                pltpu.VMEM((q_count, m_all), jnp.int32),
                pltpu.VMEM((1, slots), jnp.int32),
                pltpu.VMEM((all_rows, dim), F32),
                pltpu.VMEM((all_rows, 1), F32),
                pltpu.VMEM((all_rows, dim), BF16),
                pltpu.VMEM((dim, all_rows), BF16),
                pltpu.VMEM((held, all_rows, rows), F32),
                pltpu.VMEM((all_rows, n_pb * rows), BF16),
                pltpu.VMEM((held, slots, rows), F32),
                pltpu.VMEM((held, slots, rows), F32),
                pltpu.VMEM((n_pb, rows, dim), BF16),
                pltpu.VMEM((n_pb, q_count, max(128, m_all)), F32),
                pltpu.VMEM((n_pa, pd, max(128, n_pb * q_count)), F32),
                pltpu.VMEM((n_pb, slots, rows), F32),
                pltpu.VMEM((half, dim, rows), F32),
                pltpu.VMEM((n_pb, dim, rows), BF16),
                pltpu.VMEM((half, dim, rows), BF16),
                pltpu.VMEM((half, dim, rows), BF16),
                pltpu.VMEM((rows, dim), BF16),
                pltpu.VMEM((n_pa, piece, dim), BF16),
                dma((slots,)), dma((5,)),
                dma((n_pb,)), dma((n_pb,)),
                dma((n_pb,)), dma((n_pb,)),
                dma((n_pa,)), dma((n_pa,)),
                dma((half,)), dma((half,)),
                dma((half,)), dma((half,)),
                dma((n_pa,)), dma((n_pa,)),
            ],
            compiler_params=pltpu.CompilerParams(collective_id=0, has_side_effects=True),
        )(
            queries, encoder_outputs.reshape(all_rows, hidden), proj_weight,
            bm25_rank[:, 0, :], dense_rank[:, 0, :], custodian,
        )
        hid_grad = lax.dot_general(
            proj_grad, proj_weight, (((1,), (1,)), ((), ())), preferred_element_type=F32)
        return query_grad, hid_grad.astype(BF16).reshape(1, slots, length, hidden)

    return jax.shard_map(
        on_device,
        mesh=mesh,
        in_specs=(
            P("pb", None),
            P("pb", "pa", None, None),
            P(),
            P("pb", "pa", None),
            P("pb", "pa", None),
            P("pb", "pa"),
        ),
        out_specs=(P(("pb", "pa"), None), P("pb", "pa", None, None)),
        check_vma=False,
    )
```

profile of v0, /device:TPU:0, one launch (start us, length us, event | category | flops | bytes accessed | tf_op | source)
XLA Modules:
  0.0 36.5 jit_solution(14935741330688377454)
XLA Ops:
  0.6 0.0 copy-start
  0.6 30.9 %shard_map.77 = (bf16[2048,128]{1,0:T(8,128)(2,1)}, f32[64,128]{1,0:T(8,128)}) custom-call(bf16[256,128]{1,0:T(8,128)(2,1)} %q_ref.1, bf16[2048,1024]{1,0:T(8,128)(2,1)} %bitcast.7, bf16[1024,128]{1,0:T(8,128)(2,1)} %w_ref.1, s32[8,64]{1,0:T(8,128)} %bitcast.8, s32[8,64]{1,0:T(8,128)} %bitcast.9, s32[1,16]{1,0:T(1,128)} %idx_ref.1), custom_call_target="tpu_custom_call" | custom-call | tf_op jit(solution)/shard_map/pallas_call | solution.py:322
  31.5 0.0 copy-done
  31.5 0.0 copy-start.1
  31.5 4.3 %convolution_convert_fusion = bf16[2048,1024]{1,0:T(8,128)(2,1)} fusion(bf16[2048,128]{1,0:T(8,128)(2,1)} %get-tuple-element.5, bf16[1024,128]{1,0:T(8,128)(2,1)S(1)} %copy-done), kind=kOutput, calls=%fused_computation | convolution fusion | flops 538968064 | bytes 4980736 | tf_op jit(solution)/shard_map/dot_general | solution.py:367
  35.9 0.0 copy-done.1
  35.9 0.6 %copy.9 = f32[64,128]{1,0:T(8,128)} copy(f32[64,128]{1,0:T(8,128)S(1)} %copy-done.1) | data formatting | bytes 65536
Async XLA Ops:
  0.6 30.9 %copy-start = (bf16[1024,128]{1,0:T(8,128)(2,1)S(1)}, bf16[1024,128]{1,0:T(8,128)(2,1)}, u32[]{:S(2)}) copy-start(bf16[1024,128]{1,0:T(8,128)(2,1)} %w_ref.1) | copy-start | bytes 786436
  31.5 4.3 %copy-start.1 = (f32[64,128]{1,0:T(8,128)S(1)}, f32[64,128]{1,0:T(8,128)}, u32[]{:S(2)}) copy-start(f32[64,128]{1,0:T(8,128)} %get-tuple-element.8) | copy-start | bytes 98308
where the time goes:
time: 36.6 us; the launch traced here: 36.5 us
  Pallas kernels  30.9 us (84%)
  matrix products  4.32 us (12%)
  between operations  0.66 us (2%)
  local copies, waits for them, and re-layouts  0.62 us (2%)
    pallas_call x1, Pallas kernels, on_device(): pl.pallas_call(functools.partial(step_kernel, n_pb, n_pa, slots, length,...  30.9 us
    dot_general x1, matrix products, on_device(): lax.dot_general(proj_grad, proj_weight, (((1,), (1,)), ((), ())), preferr...  4.32 us

commit v1 on v0

--- a/solution.py
+++ b/solution.py
@@ -54,8 +54,8 @@
 def step_kernel(
     n_pb, n_pa, slots, length, pd, tokens,
     q_ref, x_ref, w_ref, bm_ref, de_ref, idx_ref,
-    pg_ref, qg_ref,
-    x_buf, w_buf, bm_buf, de_buf, idx_buf,
+    pg_ref, qg_ref, w_buf,
+    x_buf, bm_buf, de_buf, idx_buf,
     unit, scale, emb, emb_t, prob, coef, lse_buf, inv_buf,
     q_buf, t_buf, t_own, t_exp, dq_keep, dq_out, dq_part, dq_in, sum_out, sum_in,
     x_sem, i_sem, q_send, q_recv, t_send, t_recv, u_send, u_recv, p_send, p_recv, d_send, d_recv, s_send, s_recv,
@@ -117,13 +117,11 @@
             (w_ref, w_buf), (q_ref, q_buf.at[0]), (bm_ref, bm_buf), (de_ref, de_buf),
             (idx_ref, idx_buf)))
     ]
-    small[2].start()
-    small[3].start()
-    small[0].start()
+    for n in (2, 3, 1, 0):
+        small[n].start()
     for k in range(slots):
         x_copy(k).start()
         if k == chunk - 1:
-            small[1].start()
             small[4].start()
 
     def project(c):
@@ -146,6 +144,10 @@
         for d in range(2, n_pb, 2):
             q_copy(d).start()
 
+    def q_forward(d):
+        q_copy(d).wait_recv()
+        q_copy(d + 1).start()
+
     def send_second():
         for d in range(1, n_pb):
             t_copy(d).wait_recv()
@@ -161,15 +163,20 @@
     small[2].wait()
     small[3].wait()
     t_buf[0, :, 0:m_all] = joined_target(bm_buf[...], de_buf[...])
+    small[1].wait()
+    send_first()
     small[0].wait()
     chunks = slots // chunk
-    first_at = max(chunks - 2, 0)
     for c in range(chunks):
         project(c)
-        if c == first_at:
-            small[1].wait()
-            small[4].wait()
-            send_first()
+        if c == max(chunks - 3, 0):
+            send_second()
+        if c == chunks - 2:
+            q_forward(2)
+        if c == chunks - 1:
+            for d in range(2 if chunks < 2 else 4, n_pb, 2):
+                q_forward(d)
+    small[4].wait()
 
     same_query = jnp.where(
         lax.broadcasted_iota(jnp.int32, (rows, rows), 0) // tokens
@@ -224,10 +231,8 @@
         return d if d < 2 else 2 + (d - 2) % ring
 
     def scores(d):
-        if d > 0:
+        if d % 2:
             q_copy(d).wait_recv()
-        if d > 1 and d % 2 == 0:
-            q_copy(d + 1).start()
         slot = slot_of(d)
         q_rows = q_buf[d]
         for k in range(slots):
@@ -259,8 +264,6 @@
     for i in range(n_pb + lag):
         if i < n_pb:
             scores(i)
-        if i == 1:
-            send_second()
         if i == lag:
             spread_targets()
         if i >= lag:
@@ -303,6 +306,20 @@
         s_copy(e).wait_send()
 
 
+def finish_kernel(parts, pg_ref, qp_ref, w_ref, qg_ref, hid_ref, hid_buf, sem):
+    size = pg_ref.shape[0] // parts
+    copies = [pltpu.make_async_copy(qp_ref, qg_ref, sem.at[parts])]
+    copies[0].start()
+    for c in range(parts):
+        part = pl.ds(c * size, size)
+        hid_buf[part, :] = nt_dot(pg_ref[part, :], w_ref[...]).astype(BF16)
+        copy = pltpu.make_async_copy(hid_buf.at[part], hid_ref.at[part], sem.at[c])
+        copy.start()
+        copies.append(copy)
+    for copy in copies:
+        copy.wait()
+
+
 def solution(mesh):
     n_pb, n_pa = mesh.shape["pb"], mesh.shape["pa"]
 
@@ -319,17 +336,17 @@
         held = 5
         vmem = pl.BlockSpec(memory_space=pltpu.VMEM)
         dma = pltpu.SemaphoreType.DMA
-        proj_grad, query_grad = pl.pallas_call(
+        proj_grad, query_part, weight = pl.pallas_call(
             functools.partial(step_kernel, n_pb, n_pa, slots, length, pd, tokens),
             out_shape=(
-                jax.ShapeDtypeStruct((all_rows, dim), BF16),
-                jax.ShapeDtypeStruct((piece, dim), F32),
+                pltpu.VMEM((all_rows, dim), BF16),
+                pltpu.VMEM((piece, dim), F32),
+                pltpu.VMEM((hidden, dim), BF16),
             ),
             in_specs=[pl.BlockSpec(memory_space=pl.ANY)] * 6,
-            out_specs=(vmem, vmem),
+            out_specs=(vmem, vmem, vmem),
             scratch_shapes=[
                 pltpu.VMEM((all_rows, hidden), BF16),
-                pltpu.VMEM((hidden, dim), BF16),
                 pltpu.VMEM((q_count, m_all), jnp.int32),
                 pltpu.VMEM((q_count, m_all), jnp.int32),
                 pltpu.VMEM((1, slots), jnp.int32),
@@ -364,9 +381,18 @@
             queries, encoder_outputs.reshape(all_rows, hidden), proj_weight,
             bm25_rank[:, 0, :], dense_rank[:, 0, :], custodian,
         )
-        hid_grad = lax.dot_general(
-            proj_grad, proj_weight, (((1,), (1,)), ((), ())), preferred_element_type=F32)
-        return query_grad, hid_grad.astype(BF16).reshape(1, slots, length, hidden)
+        parts = 8 if slots % 8 == 0 else 1
+        query_grad, hid_grad = pl.pallas_call(
+            functools.partial(finish_kernel, parts),
+            out_shape=(
+                jax.ShapeDtypeStruct((piece, dim), F32),
+                jax.ShapeDtypeStruct((all_rows, hidden), BF16),
+            ),
+            in_specs=[vmem] * 3,
+            out_specs=(pl.BlockSpec(memory_space=pl.ANY),) * 2,
+            scratch_shapes=[pltpu.VMEM((all_rows, hidden), BF16), dma((parts + 1,))],
+        )(*(pltpu.with_memory_space_constraint(x, pltpu.VMEM) for x in (proj_grad, query_part, weight)))
+        return query_grad, hid_grad.reshape(1, slots, length, hidden)
 
     return jax.shard_map(
         on_device,

time: 36.6 us -> 32.9 us (0.90)
  matrix products: 4.32 us -> 0 us
  Pallas kernels: 30.9 us -> 32.1 us
  local copies, waits for them, and re-layouts: 0.62 us -> 0 us
    dot_general x1 -> x0, matrix products: 4.32 us -> none  [on_device(): lax.dot_general(proj_grad, proj_weight, (((1,), (1,)), ((), ())), preferr...]
    pallas_call x0 -> x1, Pallas kernels: none -> 2.38 us  [on_device(): pl.pallas_call(functools.partial(finish_kernel, parts), out_shape=(jax.Sh...]
    pallas_call x1, Pallas kernels: 30.9 us -> 29.7 us  [on_device(): pl.pallas_call(functools.partial(step_kernel, n_pb, n_pa, slots, length,...]
    unnamed x5 -> x0, local copies, waits for them, and re-layouts: 0.62 us -> none
where the time goes in v1:
time: 32.9 us; the launch traced here: 32.7 us
  Pallas kernels  32.1 us (98%)
  between operations  0.64 us (2%)
    pallas_call x1, Pallas kernels, on_device(): pl.pallas_call(functools.partial(step_kernel, n_pb, n_pa, slots, length,...  29.7 us
    pallas_call x1, Pallas kernels, on_device(): pl.pallas_call(functools.partial(finish_kernel, parts), out_shape=(jax.Sh...  2.38 us

profile of v1, /device:TPU:0, one launch (start us, length us, event | category | flops | bytes accessed | tf_op | source)
XLA Modules:
  0.0 32.7 jit_solution(4141032907084243009)
XLA Ops:
  0.6 29.7 %shard_map.77 = (bf16[2048,128]{1,0:T(8,128)(2,1)S(1)}, f32[64,128]{1,0:T(8,128)S(1)}, bf16[1024,128]{1,0:T(8,128)(2,1)S(1)}) custom-call(bf16[256,128]{1,0:T(8,128)(2,1)} %q_ref.1, bf16[2048,1024]{1,0:T(8,128)(2,1)} %bitcast.4, bf16[1024,128]{1,0:T(8,128)(2,1)} %w_ref.1, s32[8,64]{1,0:T(8,128)} %bitcast.5, s32[8,64]{1,0:T(8,128)} %bitcast.6, s32[1,16]{1,0:T(1,128)} %idx_ref.1), custom_call_target="tpu_custom_call" | custom-call | tf_op jit(solution)/shard_map/pallas_call | solution.py:339
  30.4 2.4 %shard_map.78 = (f32[64,128]{1,0:T(8,128)}, bf16[2048,1024]{1,0:T(8,128)(2,1)}) custom-call(bf16[2048,128]{1,0:T(8,128)(2,1)S(1)} %get-tuple-element.7.pg_ref, f32[64,128]{1,0:T(8,128)S(1)} %get-tuple-element.8.qp_ref, bf16[1024,128]{1,0:T(8,128)(2,1)S(1)} %get-tuple-element.9.w_ref), custom_call_target="tpu_custom_call" | custom-call | tf_op jit(solution)/shard_map/pallas_call | solution.py:385

commit v2 on v1

--- a/solution.py
+++ b/solution.py
@@ -55,9 +55,9 @@
     n_pb, n_pa, slots, length, pd, tokens,
     q_ref, x_ref, w_ref, bm_ref, de_ref, idx_ref,
     pg_ref, qg_ref, w_buf,
-    x_buf, bm_buf, de_buf, idx_buf,
-    unit, scale, emb, emb_t, prob, coef, lse_buf, inv_buf,
-    q_buf, t_buf, t_own, t_exp, dq_keep, dq_out, dq_part, dq_in, sum_out, sum_in,
+    x_buf, rank_buf, idx_buf,
+    unit, scale, emb, emb_t, prob, coef, lse_buf, inv_buf, factor_buf,
+    q_buf, t_own, t_exp, dq_keep, dq_out, dq_part, dq_in, sum_out, sum_in,
     x_sem, i_sem, q_send, q_recv, t_send, t_recv, u_send, u_recv, p_send, p_recv, d_send, d_recv, s_send, s_recv,
 ):
     b = lax.axis_index("pb")
@@ -65,45 +65,50 @@
     rows = q_ref.shape[0]
     q_count, m_all = bm_ref.shape
     piece = rows // n_pa
-    chunk = 4 if slots % 4 == 0 else 1
-
-    def x_copy(k):
-        part = pl.ds(k * length, length)
-        return pltpu.make_async_copy(x_ref.at[part], x_buf.at[part], x_sem.at[k])
+    chunk = slots // x_sem.shape[0]
+
+    def x_copy(c):
+        part = pl.ds(c * chunk * length, chunk * length)
+        return pltpu.make_async_copy(x_ref.at[part], x_buf.at[part], x_sem.at[c])
 
     def q_copy(d):
         return pltpu.make_async_remote_copy(
-            q_buf.at[d - 1 if d % 2 else 0], q_buf.at[d], q_send.at[d], q_recv.at[d],
+            q_buf.at[d - 1 if d % 2 else 0], q_buf.at[d], q_send.at[0], q_recv.at[d],
             device_id={"pb": xor(b, 1 if d % 2 else d, n_pb)}, device_id_type=MESH)
 
     def t_copy(d):
         return pltpu.make_async_remote_copy(
-            t_buf.at[0], t_buf.at[d], t_send.at[d], t_recv.at[d],
+            rank_buf.at[0], rank_buf.at[d], t_send.at[0], t_recv.at[0],
             device_id={"pb": xor(b, d, n_pb)}, device_id_type=MESH)
 
     def u_copy(e):
         return pltpu.make_async_remote_copy(
-            t_own.at[0], t_own.at[e], u_send.at[e], u_recv.at[e],
+            t_own.at[0], t_own.at[e], u_send.at[0], u_recv.at[0],
             device_id={"pa": (o + e) % n_pa}, device_id_type=MESH)
 
     def p_copy(d):
         h = d // 2
         return pltpu.make_async_remote_copy(
-            dq_out.at[d], dq_part.at[h], p_send.at[h], p_recv.at[h],
+            dq_out.at[d], dq_part.at[h], p_send.at[0], p_recv.at[h],
             device_id={"pb": xor(b, 1, n_pb)}, device_id_type=MESH)
 
     def d_copy(d):
         h = d // 2
         return pltpu.make_async_remote_copy(
-            dq_out.at[d], dq_in.at[h], d_send.at[h], d_recv.at[h],
+            dq_out.at[d], dq_in.at[h], d_send.at[0], d_recv.at[0],
             device_id={"pb": xor(b, d, n_pb)}, device_id_type=MESH)
 
     def s_copy(e):
         to = (o + e) % n_pa
         return pltpu.make_async_remote_copy(
             sum_out.at[pl.ds(pl.multiple_of(to * piece, piece), piece)],
-            sum_in.at[e], s_send.at[e], s_recv.at[e],
+            sum_in.at[e], s_send.at[0], s_recv.at[0],
             device_id={"pa": to}, device_id_type=MESH)
+
+    def all_of(buffer, count, sem, first=1):
+        if count > first:
+            span = buffer.at[pl.ds(first, count - first)]
+            pltpu.make_async_copy(span, span, sem.at[0]).wait()
 
     barrier = pltpu.get_barrier_semaphore()
     for d in range(1, n_pb):
@@ -111,24 +116,35 @@
     for e in range(1, n_pa):
         pl.semaphore_signal(barrier, inc=1, device_id={"pa": (o + e) % n_pa}, device_id_type=MESH)
 
+    def send_first():
+        for n in (2, 3, 1):
+            small[n].wait()
+        pl.semaphore_wait(barrier, n_pb + n_pa - 2)
+        for d in range(1, n_pb):
+            t_copy(d).start()
+        q_copy(1).start()
+        for d in range(2, n_pb, 2):
+            q_copy(d).start()
+
     small = [
         pltpu.make_async_copy(src, dst, i_sem.at[n])
         for n, (src, dst) in enumerate((
-            (w_ref, w_buf), (q_ref, q_buf.at[0]), (bm_ref, bm_buf), (de_ref, de_buf),
+            (w_ref, w_buf), (q_ref, q_buf.at[0]), (bm_ref, rank_buf.at[0, 0]), (de_ref, rank_buf.at[0, 1]),
             (idx_ref, idx_buf)))
     ]
     for n in (2, 3, 1, 0):
         small[n].start()
-    for k in range(slots):
-        x_copy(k).start()
-        if k == chunk - 1:
-            small[4].start()
+    for c in range(slots // chunk):
+        x_copy(c).start()
+    small[4].start()
+    send_first()
 
     def project(c):
         part = pl.ds(c * chunk * length, chunk * length)
-        for k in range(c * chunk, (c + 1) * chunk):
-            x_copy(k).wait()
-        projected = nn_dot(x_buf[part, :], w_buf[...])
+        x_copy(c).wait()
+        half = chunk * length // 2
+        projected = jnp.concatenate(
+            [nn_dot(x_buf[pl.ds(c * chunk * length + h * half, half), :], w_buf[...]) for h in range(2)], axis=0)
         scaling = lax.rsqrt(jnp.sum(projected * projected, axis=1, keepdims=True) + norm_eps)
         unit_c = projected * scaling
         unit[part, :] = unit_c
@@ -136,46 +152,25 @@
         emb[part, :] = unit_c.astype(BF16)
         emb_t[:, part] = jnp.transpose(unit_c).astype(BF16)
 
-    def send_first():
-        pl.semaphore_wait(barrier, n_pb + n_pa - 2)
-        for d in range(1, n_pb):
-            t_copy(d).start()
-        q_copy(1).start()
-        for d in range(2, n_pb, 2):
-            q_copy(d).start()
-
     def q_forward(d):
         q_copy(d).wait_recv()
         q_copy(d + 1).start()
 
     def send_second():
-        for d in range(1, n_pb):
-            t_copy(d).wait_recv()
+        all_of(rank_buf, n_pb, t_recv)
         row = lax.broadcasted_iota(jnp.int32, (pd, m_all), 0)
         at = lax.broadcasted_iota(jnp.int32, (pd, m_all), 1)
         pick = jnp.where(at == row + b * pd, 1.0, 0.0).astype(BF16)
-        table = t_buf[:, :, 0:m_all].reshape(n_pb * q_count, m_all)
+        table = joined_target(rank_buf[:, 0], rank_buf[:, 1]).reshape(n_pb * q_count, m_all)
         first, second, third = three_parts(table)
         t_own[0, :, 0:n_pb * q_count] = nt_dot(pick, first) + nt_dot(pick, second) + nt_dot(pick, third)
         for e in range(1, n_pa):
             u_copy(e).start()
 
-    small[2].wait()
-    small[3].wait()
-    t_buf[0, :, 0:m_all] = joined_target(bm_buf[...], de_buf[...])
-    small[1].wait()
-    send_first()
     small[0].wait()
     chunks = slots // chunk
     for c in range(chunks):
         project(c)
-        if c == max(chunks - 3, 0):
-            send_second()
-        if c == chunks - 2:
-            q_forward(2)
-        if c == chunks - 1:
-            for d in range(2 if chunks < 2 else 4, n_pb, 2):
-                q_forward(d)
     small[4].wait()
 
     same_query = jnp.where(
@@ -198,15 +193,17 @@
         lse[pl.ds(k, 1), :] = largest * inv_temp + jnp.log(total)
         inv[pl.ds(k, 1), :] = 1.0 / total
 
-    def factor_of(d, lse, inv):
-        first, second, third = three_parts(lse[...])
-        score = nn_dot(first, same_query) + nn_dot(second, same_query) + nn_dot(third, same_query)
-        residual = (score * (tau / tokens) - t_exp[d]).astype(BF16).astype(F32)
-        return jnp.where(filled, residual * (1.0 / tokens) * inv[...], 0.0)
+    def set_factors(ds):
+        parts = [part.astype(F32) for d in ds for part in three_parts(lse_buf[slot_of(d)])]
+        sums = nn_dot(jnp.concatenate(parts, axis=0).astype(BF16), same_query)
+        for n, d in enumerate(ds):
+            first, second, third = (sums[(3 * n + p) * slots:(3 * n + p + 1) * slots] for p in range(3))
+            score = first + second + third
+            residual = (score * (tau / tokens) - t_exp[d]).astype(BF16).astype(F32)
+            factor_buf[slot_of(d)] = jnp.where(filled, residual * (1.0 / tokens) * inv_buf[slot_of(d)], 0.0)
 
     def spread_targets():
-        for e in range(1, n_pa):
-            u_copy(e).wait_recv()
+        all_of(t_own, n_pa, u_recv)
         row = lax.broadcasted_iota(jnp.int32, (slots, pd), 1)
         picked = jnp.zeros((slots, n_pb * q_count), F32)
         for e in range(n_pa):
@@ -223,87 +220,118 @@
             wide = nn_dot(picked_parts, spread)
             t_exp[d] = wide[0:slots] + wide[slots:2 * slots] + wide[2 * slots:3 * slots]
 
-    grad_order = list(range(2, n_pb)) + [1, 0]
-    ring = prob.shape[0] - 2
-    lag = ring + 1
+    new_order = [0, 1] + list(range(2, n_pb, 2)) + list(range(3, n_pb, 2))
+    wanted = [d + odd for odd in (0, 1) for d in [n_pb - 2] + list(range(2, n_pb - 2, 2))] + [1, 0]
+    free = list(range(prob.shape[0]))
+    lag = len(free) - 1
+    slot_at = {}
+    done = []
+
+    group = 2 if slots % 2 == 0 else 1
 
     def slot_of(d):
-        return d if d < 2 else 2 + (d - 2) % ring
-
-    def scores(d):
-        if d % 2:
-            q_copy(d).wait_recv()
-        slot = slot_of(d)
-        q_rows = q_buf[d]
-        for k in range(slots):
-            score_slot(k, q_rows, prob.at[slot], lse_buf.at[slot], inv_buf.at[slot])
+        return slot_at[d]
+
+    def keeps(d):
+        return d == 0 or (d > 1 and d % 2 == 1)
+
+    def step(new, old, ready):
+        if ready:
+            set_factors(ready)
+        if old is not None:
+            lanes = pl.ds(old * rows, rows)
+            factor = factor_buf[slot_of(old)]
+        dq = None
+        for first in range(0, slots, group):
+            for k in range(first, first + group):
+                part = pl.ds(k * length, length)
+                if new is not None:
+                    at = slot_of(new)
+                    score_slot(k, q_buf[new], prob.at[at], lse_buf.at[at], inv_buf.at[at])
+                if old is not None:
+                    coef[part, lanes] = (prob[slot_of(old), part, :] * factor[k:k + 1, :]).astype(BF16)
+            if old is not None:
+                span = pl.ds(first * length, group * length)
+                more = nn_dot(emb_t[:, span], coef[span, lanes])
+                dq = more if dq is None else dq + more
+        if old is not None:
+            if keeps(old):
+                dq_keep[old // 2] = dq
+            else:
+                dq_out[old] = dq.astype(BF16)
+                p_copy(old).start()
 
     def finish_pair(d):
-        p_copy(d + 1).wait_recv()
+        p_copy(d - 1).wait_recv()
         dq_out[d] = (dq_keep[d // 2] + dq_part[d // 2].astype(F32)).astype(BF16)
         d_copy(d).start()
 
-    def grads(i):
-        d = grad_order[i]
-        slot = slot_of(d)
-        factor = factor_of(d, lse_buf.at[slot], inv_buf.at[slot])
-        lanes = pl.ds(d * rows, rows)
-        for k in range(slots):
-            part = pl.ds(k * length, length)
-            coef[part, lanes] = (prob[slot, part, :] * factor[k:k + 1, :]).astype(BF16)
-        dq = nn_dot(emb_t[...], coef[:, lanes])
-        if d % 2:
-            dq_out[d] = dq.astype(BF16)
-            p_copy(d).start()
-        else:
-            dq_keep[d // 2] = dq
-        before = grad_order[i - 1]
-        if i > 0 and before % 2 and before > 1:
-            finish_pair(before - 1)
-
+    ready = []
     for i in range(n_pb + lag):
-        if i < n_pb:
-            scores(i)
+        new = new_order[i] if i < n_pb else None
+        if new is not None and new > 2 and new % 2:
+            q_copy(new).wait_recv()
+        elif new == 1:
+            q_copy(1).wait_recv()
+        elif new == 2:
+            q_forward(2)
+            if n_pb > 4:
+                q_forward(4)
+        elif new is not None and new > 2 and new + 2 < n_pb:
+            q_forward(new + 2)
+        if i == 2:
+            send_second()
         if i == lag:
             spread_targets()
+        old = None
         if i >= lag:
-            grads(i - lag)
+            old = next(d for d in wanted if d in slot_at and d not in done)
+        if new is not None:
+            slot_at[new] = free.pop(0)
+        step(new, old, ready if i >= lag else [])
+        if i >= lag:
+            ready = []
+            done.append(old)
+            free.append(slot_at[old])
+            if old > 1 and old ^ 1 in done:
+                finish_pair(old | 1)
+        if new is not None:
+            ready.append(new)
+
     def passage_grad(c):
         part = pl.ds(c * chunk * length, chunk * length)
         q_all = q_buf[...].reshape(n_pb * rows, q_ref.shape[1])
-        slot_grad = nn_dot(coef[part, :], q_all).astype(BF16).astype(F32)
+        half = chunk * length // 2
+        slot_grad = jnp.concatenate(
+            [nn_dot(coef[pl.ds(c * chunk * length + h * half, half), :], q_all) for h in range(2)], axis=0)
+        slot_grad = slot_grad.astype(BF16).astype(F32)
         unit_c = unit[part, :]
         inner = jnp.sum(unit_c * slot_grad, axis=1, keepdims=True)
         pg_ref[part, :] = ((slot_grad - unit_c * inner) * scale[part, :]).astype(BF16)
 
-    for c in range(chunks // 4):
+    for c in range(chunks - 1):
         passage_grad(c)
     p_copy(1).wait_recv()
     total = dq_keep[0] + dq_part[0].astype(F32)
-    for d in range(n_pb - 2, 0, -2):
-        d_copy(d).wait_recv()
-        total = total + dq_in[d // 2].astype(F32)
+    all_of(dq_in, n_pb // 2, d_recv)
+    for h in range(1, n_pb // 2):
+        total = total + dq_in[h].astype(F32)
     sum_out[...] = jnp.transpose(total).astype(BF16)
     for e in range(1, n_pa):
         s_copy(e).start()
-    for c in range(chunks // 4, chunks):
-        passage_grad(c)
+    passage_grad(chunks - 1)
     mine = sum_out[pl.ds(pl.multiple_of(o * piece, piece), piece), :].astype(F32)
+    all_of(sum_in, n_pa, s_recv)
     for e in range(1, n_pa):
-        s_copy(e).wait_recv()
         mine = mine + sum_in[e].astype(F32)
     qg_ref[...] = mine
 
-    for d in range(1, n_pb):
-        t_copy(d).wait_send()
-        q_copy(d).wait_send()
-        if d % 2:
-            p_copy(d).wait_send()
-        else:
-            d_copy(d).wait_send()
-    for e in range(1, n_pa):
-        u_copy(e).wait_send()
-        s_copy(e).wait_send()
+    all_of(rank_buf, n_pb, t_send)
+    all_of(q_buf, n_pb, q_send)
+    all_of(t_own, n_pa, u_send)
+    all_of(dq_part, n_pb // 2, p_send, 0)
+    all_of(dq_in, n_pb // 2, d_send)
+    all_of(sum_in, n_pa, s_send)
 
 
 def finish_kernel(parts, pg_ref, qp_ref, w_ref, qg_ref, hid_ref, hid_buf, sem):
@@ -333,7 +361,8 @@
         all_rows = slots * length
         piece = rows // n_pa
         half = n_pb // 2
-        held = 5
+        chunk = 4 if slots % 4 == 0 else 1
+        held = min(8, n_pb)
         vmem = pl.BlockSpec(memory_space=pltpu.VMEM)
         dma = pltpu.SemaphoreType.DMA
         proj_grad, query_part, weight = pl.pallas_call(
@@ -347,8 +376,7 @@
             out_specs=(vmem, vmem, vmem),
             scratch_shapes=[
                 pltpu.VMEM((all_rows, hidden), BF16),
-                pltpu.VMEM((q_count, m_all), jnp.int32),
-                pltpu.VMEM((q_count, m_all), jnp.int32),
+                pltpu.VMEM((n_pb, 2, q_count, m_all), jnp.int32),
                 pltpu.VMEM((1, slots), jnp.int32),
                 pltpu.VMEM((all_rows, dim), F32),
                 pltpu.VMEM((all_rows, 1), F32),
@@ -358,8 +386,8 @@
                 pltpu.VMEM((all_rows, n_pb * rows), BF16),
                 pltpu.VMEM((held, slots, rows), F32),
                 pltpu.VMEM((held, slots, rows), F32),
+                pltpu.VMEM((held, slots, rows), F32),
                 pltpu.VMEM((n_pb, rows, dim), BF16),
-                pltpu.VMEM((n_pb, q_count, max(128, m_all)), F32),
                 pltpu.VMEM((n_pa, pd, max(128, n_pb * q_count)), F32),
                 pltpu.VMEM((n_pb, slots, rows), F32),
                 pltpu.VMEM((half, dim, rows), F32),
@@ -368,13 +396,13 @@
                 pltpu.VMEM((half, dim, rows), BF16),
                 pltpu.VMEM((rows, dim), BF16),
                 pltpu.VMEM((n_pa, piece, dim), BF16),
-                dma((slots,)), dma((5,)),
-                dma((n_pb,)), dma((n_pb,)),
-                dma((n_pb,)), dma((n_pb,)),
-                dma((n_pa,)), dma((n_pa,)),
-                dma((half,)), dma((half,)),
-                dma((half,)), dma((half,)),
-                dma((n_pa,)), dma((n_pa,)),
+                dma((slots // chunk,)), dma((5,)),
+                dma((1,)), dma((n_pb,)),
+                dma((1,)), dma((1,)),
+                dma((1,)), dma((1,)),
+                dma((1,)), dma((half,)),
+                dma((1,)), dma((1,)),
+                dma((1,)), dma((1,)),
             ],
             compiler_params=pltpu.CompilerParams(collective_id=0, has_side_effects=True),
         )(

time: 32.9 us -> 29.5 us (0.90)
  Pallas kernels: 32.1 us -> 28.7 us
    pallas_call x1, Pallas kernels: 29.7 us -> 26.3 us  [on_device(): pl.pallas_call(functools.partial(step_kernel, n_pb, n_pa, slots, length,...]
where the time goes in v2:
time: 29.5 us; the launch traced here: 29.3 us
  Pallas kernels  28.7 us (97%)
  between operations  0.64 us (2%)
    pallas_call x1, Pallas kernels, on_device(): pl.pallas_call(functools.partial(step_kernel, n_pb, n_pa, slots, length,...  26.3 us
    pallas_call x1, Pallas kernels, on_device(): pl.pallas_call(functools.partial(finish_kernel, parts), out_shape=(jax.Sh...  2.38 us

profile of v2, /device:TPU:0, one launch (start us, length us, event | category | flops | bytes accessed | tf_op | source)
XLA Modules:
  0.0 29.3 jit_solution(6926079293319257961)
XLA Ops:
  0.6 26.3 %shard_map.77 = (bf16[2048,128]{1,0:T(8,128)(2,1)S(1)}, f32[64,128]{1,0:T(8,128)S(1)}, bf16[1024,128]{1,0:T(8,128)(2,1)S(1)}) custom-call(bf16[256,128]{1,0:T(8,128)(2,1)} %q_ref.1, bf16[2048,1024]{1,0:T(8,128)(2,1)} %bitcast.4, bf16[1024,128]{1,0:T(8,128)(2,1)} %w_ref.1, s32[8,64]{1,0:T(8,128)} %bitcast.5, s32[8,64]{1,0:T(8,128)} %bitcast.6, s32[1,16]{1,0:T(1,128)} %idx_ref.1), custom_call_target="tpu_custom_call" | custom-call | tf_op jit(solution)/shard_map/pallas_call | solution.py:368
  27.0 2.4 %shard_map.78 = (f32[64,128]{1,0:T(8,128)}, bf16[2048,1024]{1,0:T(8,128)(2,1)}) custom-call(bf16[2048,128]{1,0:T(8,128)(2,1)S(1)} %get-tuple-element.7.pg_ref, f32[64,128]{1,0:T(8,128)S(1)} %get-tuple-element.8.qp_ref, bf16[1024,128]{1,0:T(8,128)(2,1)S(1)} %get-tuple-element.9.w_ref), custom_call_target="tpu_custom_call" | custom-call | tf_op jit(solution)/shard_map/pallas_call | solution.py:413

commit v3 on v2

--- a/solution.py
+++ b/solution.py
@@ -57,7 +57,7 @@
     pg_ref, qg_ref, w_buf,
     x_buf, rank_buf, idx_buf,
     unit, scale, emb, emb_t, prob, coef, lse_buf, inv_buf, factor_buf,
-    q_buf, t_own, t_exp, dq_keep, dq_out, dq_part, dq_in, sum_out, sum_in,
+    q_buf, t_out, t_in, t_exp, dq_keep, dq_out, dq_part, far_out, far_in, sum_out, sum_in,
     x_sem, i_sem, q_send, q_recv, t_send, t_recv, u_send, u_recv, p_send, p_recv, d_send, d_recv, s_send, s_recv,
 ):
     b = lax.axis_index("pb")
@@ -76,15 +76,15 @@
             q_buf.at[d - 1 if d % 2 else 0], q_buf.at[d], q_send.at[0], q_recv.at[d],
             device_id={"pb": xor(b, 1 if d % 2 else d, n_pb)}, device_id_type=MESH)
 
-    def t_copy(d):
-        return pltpu.make_async_remote_copy(
-            rank_buf.at[0], rank_buf.at[d], t_send.at[0], t_recv.at[0],
+    def t_copy(e):
+        return pltpu.make_async_remote_copy(
+            rank_buf.at[0], rank_buf.at[e], t_send.at[0], t_recv.at[0],
+            device_id={"pa": (o + e) % n_pa}, device_id_type=MESH)
+
+    def u_copy(d):
+        return pltpu.make_async_remote_copy(
+            t_out.at[d], t_in.at[d], u_send.at[0], u_recv.at[0],
             device_id={"pb": xor(b, d, n_pb)}, device_id_type=MESH)
-
-    def u_copy(e):
-        return pltpu.make_async_remote_copy(
-            t_own.at[0], t_own.at[e], u_send.at[0], u_recv.at[0],
-            device_id={"pa": (o + e) % n_pa}, device_id_type=MESH)
 
     def p_copy(d):
         h = d // 2
@@ -92,11 +92,12 @@
             dq_out.at[d], dq_part.at[h], p_send.at[0], p_recv.at[h],
             device_id={"pb": xor(b, 1, n_pb)}, device_id_type=MESH)
 
-    def d_copy(d):
-        h = d // 2
-        return pltpu.make_async_remote_copy(
-            dq_out.at[d], dq_in.at[h], d_send.at[0], d_recv.at[0],
-            device_id={"pb": xor(b, d, n_pb)}, device_id_type=MESH)
+    def d_copy(d, e):
+        to = (o + e) % n_pa
+        return pltpu.make_async_remote_copy(
+            far_out.at[d // 2, pl.ds(pl.multiple_of(to * piece, piece), piece)],
+            far_in.at[d // 2, e], d_send.at[0], d_recv.at[0],
+            device_id={"pb": xor(b, d, n_pb), "pa": to}, device_id_type=MESH)
 
     def s_copy(e):
         to = (o + e) % n_pa
@@ -120,8 +121,8 @@
         for n in (2, 3, 1):
             small[n].wait()
         pl.semaphore_wait(barrier, n_pb + n_pa - 2)
-        for d in range(1, n_pb):
-            t_copy(d).start()
+        for e in range(1, n_pa):
+            t_copy(e).start()
         q_copy(1).start()
         for d in range(2, n_pb, 2):
             q_copy(d).start()
@@ -140,11 +141,15 @@
     send_first()
 
     def project(c):
+        size = chunk * length // 2
+        x_copy(c).wait()
+        for h in range(2):
+            part = pl.ds((2 * c + h) * size, size)
+            unit[part, :] = nn_dot(x_buf[part, :], w_buf[...])
+
+    def normalize(c):
         part = pl.ds(c * chunk * length, chunk * length)
-        x_copy(c).wait()
-        half = chunk * length // 2
-        projected = jnp.concatenate(
-            [nn_dot(x_buf[pl.ds(c * chunk * length + h * half, half), :], w_buf[...]) for h in range(2)], axis=0)
+        projected = unit[part, :]
         scaling = lax.rsqrt(jnp.sum(projected * projected, axis=1, keepdims=True) + norm_eps)
         unit_c = projected * scaling
         unit[part, :] = unit_c
@@ -152,25 +157,31 @@
         emb[part, :] = unit_c.astype(BF16)
         emb_t[:, part] = jnp.transpose(unit_c).astype(BF16)
 
+    def send_second():
+        all_of(rank_buf, n_pa, t_recv)
+        row = lax.broadcasted_iota(jnp.int32, (n_pb * pd, m_all), 0)
+        at = lax.broadcasted_iota(jnp.int32, (n_pb * pd, m_all), 1)
+        pick = jnp.where(at == xor(row // pd, b, n_pb) * pd + row % pd, 1.0, 0.0).astype(BF16)
+        table = joined_target(rank_buf[:, 0], rank_buf[:, 1]).reshape(n_pa * q_count, m_all)
+        first, second, third = three_parts(table)
+        picked = nt_dot(pick, first) + nt_dot(pick, second) + nt_dot(pick, third)
+        for d in range(n_pb):
+            to = t_out if d > 0 else t_in
+            to[d, :, 0:n_pa * q_count] = picked[d * pd:(d + 1) * pd]
+        for d in range(1, n_pb):
+            u_copy(d).start()
+
     def q_forward(d):
         q_copy(d).wait_recv()
         q_copy(d + 1).start()
-
-    def send_second():
-        all_of(rank_buf, n_pb, t_recv)
-        row = lax.broadcasted_iota(jnp.int32, (pd, m_all), 0)
-        at = lax.broadcasted_iota(jnp.int32, (pd, m_all), 1)
-        pick = jnp.where(at == row + b * pd, 1.0, 0.0).astype(BF16)
-        table = joined_target(rank_buf[:, 0], rank_buf[:, 1]).reshape(n_pb * q_count, m_all)
-        first, second, third = three_parts(table)
-        t_own[0, :, 0:n_pb * q_count] = nt_dot(pick, first) + nt_dot(pick, second) + nt_dot(pick, third)
-        for e in range(1, n_pa):
-            u_copy(e).start()
 
     small[0].wait()
     chunks = slots // chunk
     for c in range(chunks):
         project(c)
+        if c > 0:
+            normalize(c - 1)
+    normalize(chunks - 1)
     small[4].wait()
 
     same_query = jnp.where(
@@ -203,25 +214,32 @@
             factor_buf[slot_of(d)] = jnp.where(filled, residual * (1.0 / tokens) * inv_buf[slot_of(d)], 0.0)
 
     def spread_targets():
-        all_of(t_own, n_pa, u_recv)
-        row = lax.broadcasted_iota(jnp.int32, (slots, pd), 1)
-        picked = jnp.zeros((slots, n_pb * q_count), F32)
-        for e in range(n_pa):
-            shard = (o - e + n_pa) % n_pa
-            one_hot = jnp.where(held == row + shard * pd, 1.0, 0.0).astype(BF16)
-            for part in three_parts(t_own[e, :, 0:n_pb * q_count]):
+        all_of(t_in, n_pb, u_recv)
+        width = n_pa * q_count
+        column = lax.broadcasted_iota(jnp.int32, (slots, pd), 1)
+        one_hot = jnp.where(held % pd == column, 1.0, 0.0).astype(BF16)
+        lane = lax.broadcasted_iota(jnp.int32, (slots, width), 1)
+        own_shard = jnp.logical_and(filled, held // pd == (o - lane // q_count + n_pa) % n_pa)
+        row_at = lax.broadcasted_iota(jnp.int32, (width, rows), 0)
+        lane_at = lax.broadcasted_iota(jnp.int32, (width, rows), 1)
+        spread = jnp.where(row_at % q_count == lane_at // tokens, 1.0, 0.0).astype(BF16)
+        parts = []
+        for d in range(n_pb):
+            picked = jnp.zeros((slots, width), F32)
+            for part in three_parts(t_in[d, :, 0:width]):
                 picked = picked + nn_dot(one_hot, part)
-        picked_parts = jnp.concatenate(
-            [p.astype(F32) for p in three_parts(picked)], axis=0).astype(BF16)
-        row_at = lax.broadcasted_iota(jnp.int32, (n_pb * q_count, rows), 0)
-        lane_at = lax.broadcasted_iota(jnp.int32, (n_pb * q_count, rows), 1)
+            parts += [part.astype(F32) for part in three_parts(jnp.where(own_shard, picked, 0.0))]
+        wide = nn_dot(jnp.concatenate(parts, axis=0).astype(BF16), spread)
         for d in range(n_pb):
-            spread = jnp.where(row_at == d * q_count + lane_at // tokens, 1.0, 0.0).astype(BF16)
-            wide = nn_dot(picked_parts, spread)
-            t_exp[d] = wide[0:slots] + wide[slots:2 * slots] + wide[2 * slots:3 * slots]
+            first, second, third = (wide[(3 * d + p) * slots:(3 * d + p + 1) * slots] for p in range(3))
+            t_exp[d] = first + second + third
 
     new_order = [0, 1] + list(range(2, n_pb, 2)) + list(range(3, n_pb, 2))
-    wanted = [d + odd for odd in (0, 1) for d in [n_pb - 2] + list(range(2, n_pb - 2, 2))] + [1, 0]
+    sent = [n_pb - 2] + list(range(2, n_pb - 2, 2))
+    wanted = sent[:1]
+    for d, after in zip(sent, sent[1:]):
+        wanted += [after, d + 1]
+    wanted += [sent[-1] + 1, 1, 0]
     free = list(range(prob.shape[0]))
     lag = len(free) - 1
     slot_at = {}
@@ -263,8 +281,9 @@
 
     def finish_pair(d):
         p_copy(d - 1).wait_recv()
-        dq_out[d] = (dq_keep[d // 2] + dq_part[d // 2].astype(F32)).astype(BF16)
-        d_copy(d).start()
+        far_out[d // 2] = jnp.transpose(dq_keep[d // 2] + dq_part[d // 2].astype(F32)).astype(BF16)
+        for e in range(n_pa):
+            d_copy(d, e).start()
 
     ready = []
     for i in range(n_pb + lag):
@@ -273,13 +292,9 @@
             q_copy(new).wait_recv()
         elif new == 1:
             q_copy(1).wait_recv()
-        elif new == 2:
-            q_forward(2)
-            if n_pb > 4:
-                q_forward(4)
-        elif new is not None and new > 2 and new + 2 < n_pb:
-            q_forward(new + 2)
-        if i == 2:
+        elif new is not None and new > 1:
+            q_forward(new)
+        if i == 1:
             send_second()
         if i == lag:
             spread_targets()
@@ -309,28 +324,28 @@
         inner = jnp.sum(unit_c * slot_grad, axis=1, keepdims=True)
         pg_ref[part, :] = ((slot_grad - unit_c * inner) * scale[part, :]).astype(BF16)
 
-    for c in range(chunks - 1):
-        passage_grad(c)
+    passage_grad(0)
     p_copy(1).wait_recv()
-    total = dq_keep[0] + dq_part[0].astype(F32)
-    all_of(dq_in, n_pb // 2, d_recv)
-    for h in range(1, n_pb // 2):
-        total = total + dq_in[h].astype(F32)
-    sum_out[...] = jnp.transpose(total).astype(BF16)
+    sum_out[...] = jnp.transpose(dq_keep[0] + dq_part[0].astype(F32)).astype(BF16)
     for e in range(1, n_pa):
         s_copy(e).start()
-    passage_grad(chunks - 1)
+    for c in range(1, chunks):
+        passage_grad(c)
     mine = sum_out[pl.ds(pl.multiple_of(o * piece, piece), piece), :].astype(F32)
     all_of(sum_in, n_pa, s_recv)
     for e in range(1, n_pa):
         mine = mine + sum_in[e].astype(F32)
+    all_of(far_in, n_pb // 2, d_recv)
+    for h in range(1, n_pb // 2):
+        for e in range(n_pa):
+            mine = mine + far_in[h, e].astype(F32)
     qg_ref[...] = mine
 
-    all_of(rank_buf, n_pb, t_send)
+    all_of(rank_buf, n_pa, t_send)
     all_of(q_buf, n_pb, q_send)
-    all_of(t_own, n_pa, u_send)
+    all_of(t_in, n_pb, u_send)
     all_of(dq_part, n_pb // 2, p_send, 0)
-    all_of(dq_in, n_pb // 2, d_send)
+    all_of(far_in, n_pb // 2, d_send)
     all_of(sum_in, n_pa, s_send)
 
 
@@ -376,7 +391,7 @@
             out_specs=(vmem, vmem, vmem),
             scratch_shapes=[
                 pltpu.VMEM((all_rows, hidden), BF16),
-                pltpu.VMEM((n_pb, 2, q_count, m_all), jnp.int32),
+                pltpu.VMEM((n_pa, 2, q_count, m_all), jnp.int32),
                 pltpu.VMEM((1, slots), jnp.int32),
                 pltpu.VMEM((all_rows, dim), F32),
                 pltpu.VMEM((all_rows, 1), F32),
@@ -388,12 +403,14 @@
                 pltpu.VMEM((held, slots, rows), F32),
                 pltpu.VMEM((held, slots, rows), F32),
                 pltpu.VMEM((n_pb, rows, dim), BF16),
-                pltpu.VMEM((n_pa, pd, max(128, n_pb * q_count)), F32),
+                pltpu.VMEM((n_pb, pd, max(128, n_pa * q_count)), F32),
+                pltpu.VMEM((n_pb, pd, max(128, n_pa * q_count)), F32),
                 pltpu.VMEM((n_pb, slots, rows), F32),
                 pltpu.VMEM((half, dim, rows), F32),
                 pltpu.VMEM((n_pb, dim, rows), BF16),
                 pltpu.VMEM((half, dim, rows), BF16),
-                pltpu.VMEM((half, dim, rows), BF16),
+                pltpu.VMEM((half, rows, dim), BF16),
+                pltpu.VMEM((half, n_pa, piece, dim), BF16),
                 pltpu.VMEM((rows, dim), BF16),
                 pltpu.VMEM((n_pa, piece, dim), BF16),
                 dma((slots // chunk,)), dma((5,)),

time: 29.5 us -> 26.9 us (0.912)
  Pallas kernels: 28.7 us -> 26 us
    pallas_call x1, Pallas kernels: 26.3 us -> 23.7 us  [on_device(): pl.pallas_call(functools.partial(step_kernel, n_pb, n_pa, slots, length,...]
where the time goes in v3:
time: 26.9 us; the launch traced here: 26.7 us
  Pallas kernels  26 us (97%)
  between operations  0.64 us (2%)
    pallas_call x1, Pallas kernels, on_device(): pl.pallas_call(functools.partial(step_kernel, n_pb, n_pa, slots, length,...  23.7 us
    pallas_call x1, Pallas kernels, on_device(): pl.pallas_call(functools.partial(finish_kernel, parts), out_shape=(jax.Sh...  2.38 us

profile of v3, /device:TPU:0, one launch (start us, length us, event | category | flops | bytes accessed | tf_op | source)
XLA Modules:
  0.0 26.7 jit_solution(9985406207746946687)
XLA Ops:
  0.6 23.7 %shard_map.77 = (bf16[2048,128]{1,0:T(8,128)(2,1)S(1)}, f32[64,128]{1,0:T(8,128)S(1)}, bf16[1024,128]{1,0:T(8,128)(2,1)S(1)}) custom-call(bf16[256,128]{1,0:T(8,128)(2,1)} %q_ref.1, bf16[2048,1024]{1,0:T(8,128)(2,1)} %bitcast.4, bf16[1024,128]{1,0:T(8,128)(2,1)} %w_ref.1, s32[8,64]{1,0:T(8,128)} %bitcast.5, s32[8,64]{1,0:T(8,128)} %bitcast.6, s32[1,16]{1,0:T(1,128)} %idx_ref.1), custom_call_target="tpu_custom_call" | custom-call | tf_op jit(solution)/shard_map/pallas_call | solution.py:383
  24.3 2.4 %shard_map.78 = (f32[64,128]{1,0:T(8,128)}, bf16[2048,1024]{1,0:T(8,128)(2,1)}) custom-call(bf16[2048,128]{1,0:T(8,128)(2,1)S(1)} %get-tuple-element.7.pg_ref, f32[64,128]{1,0:T(8,128)S(1)} %get-tuple-element.8.qp_ref, bf16[1024,128]{1,0:T(8,128)(2,1)S(1)} %get-tuple-element.9.w_ref), custom_call_target="tpu_custom_call" | custom-call | tf_op jit(solution)/shard_map/pallas_call | solution.py:430

commit v4 on v3

--- a/solution.py
+++ b/solution.py
@@ -54,7 +54,7 @@
 def step_kernel(
     n_pb, n_pa, slots, length, pd, tokens,
     q_ref, x_ref, w_ref, bm_ref, de_ref, idx_ref,
-    pg_ref, qg_ref, w_buf,
+    pg_ref, qg_ref, w_buf, hid_ref,
     x_buf, rank_buf, idx_buf,
     unit, scale, emb, emb_t, prob, coef, lse_buf, inv_buf, factor_buf,
     q_buf, t_out, t_in, t_exp, dq_keep, dq_out, dq_part, far_out, far_in, sum_out, sum_in,
@@ -239,7 +239,9 @@
     wanted = sent[:1]
     for d, after in zip(sent, sent[1:]):
         wanted += [after, d + 1]
-    wanted += [sent[-1] + 1, 1, 0]
+    wanted += [sent[-1] + 1]
+    wanted = [d for d in wanted if d % 2 == 0] + [d for d in wanted if d % 2]
+    wanted = wanted[:-1] + [1] + wanted[-1:] + [0]
     free = list(range(prob.shape[0]))
     lag = len(free) - 1
     slot_at = {}
@@ -279,6 +281,12 @@
                 dq_out[old] = dq.astype(BF16)
                 p_copy(old).start()
 
+    def finish_own():
+        p_copy(1).wait_recv()
+        sum_out[...] = jnp.transpose(dq_keep[0] + dq_part[0].astype(F32)).astype(BF16)
+        for e in range(1, n_pa):
+            s_copy(e).start()
+
     def finish_pair(d):
         p_copy(d - 1).wait_recv()
         far_out[d // 2] = jnp.transpose(dq_keep[d // 2] + dq_part[d // 2].astype(F32)).astype(BF16)
@@ -303,13 +311,15 @@
             old = next(d for d in wanted if d in slot_at and d not in done)
         if new is not None:
             slot_at[new] = free.pop(0)
-        step(new, old, ready if i >= lag else [])
         if i >= lag:
-            ready = []
+            first = [d for d in ready if i > lag or d == old]
+            ready = [d for d in ready if d not in first]
+        step(new, old, first if i >= lag else [])
+        if i >= lag:
             done.append(old)
             free.append(slot_at[old])
-            if old > 1 and old ^ 1 in done:
-                finish_pair(old | 1)
+            if old ^ 1 in done:
+                finish_pair(old | 1) if old > 1 else finish_own()
         if new is not None:
             ready.append(new)
 
@@ -324,13 +334,12 @@
         inner = jnp.sum(unit_c * slot_grad, axis=1, keepdims=True)
         pg_ref[part, :] = ((slot_grad - unit_c * inner) * scale[part, :]).astype(BF16)
 
-    passage_grad(0)
-    p_copy(1).wait_recv()
-    sum_out[...] = jnp.transpose(dq_keep[0] + dq_part[0].astype(F32)).astype(BF16)
-    for e in range(1, n_pa):
-        s_copy(e).start()
-    for c in range(1, chunks):
+    for c in range(chunks):
         passage_grad(c)
+    first_rows = hid_ref.shape[0] // 2
+    for h in range(2):
+        part = pl.ds(h * first_rows, first_rows)
+        hid_ref[part, :] = nt_dot(pg_ref[part, :], w_buf[...]).astype(BF16)
     mine = sum_out[pl.ds(pl.multiple_of(o * piece, piece), piece), :].astype(F32)
     all_of(sum_in, n_pa, s_recv)
     for e in range(1, n_pa):
@@ -349,11 +358,15 @@
     all_of(sum_in, n_pa, s_send)
 
 
-def finish_kernel(parts, pg_ref, qp_ref, w_ref, qg_ref, hid_ref, hid_buf, sem):
+def finish_kernel(parts, pg_ref, qp_ref, w_ref, first_ref, qg_ref, hid_ref, hid_buf, sem):
     size = pg_ref.shape[0] // parts
-    copies = [pltpu.make_async_copy(qp_ref, qg_ref, sem.at[parts])]
-    copies[0].start()
-    for c in range(parts):
+    ready = first_ref.shape[0] // size
+    copies = [
+        pltpu.make_async_copy(first_ref, hid_ref.at[pl.ds(0, ready * size)], sem.at[0]),
+        pltpu.make_async_copy(qp_ref, qg_ref, sem.at[parts])]
+    for copy in copies:
+        copy.start()
+    for c in range(ready, parts):
         part = pl.ds(c * size, size)
         hid_buf[part, :] = nt_dot(pg_ref[part, :], w_ref[...]).astype(BF16)
         copy = pltpu.make_async_copy(hid_buf.at[part], hid_ref.at[part], sem.at[c])
@@ -380,15 +393,16 @@
         held = min(8, n_pb)
         vmem = pl.BlockSpec(memory_space=pltpu.VMEM)
         dma = pltpu.SemaphoreType.DMA
-        proj_grad, query_part, weight = pl.pallas_call(
+        handed = pl.pallas_call(
             functools.partial(step_kernel, n_pb, n_pa, slots, length, pd, tokens),
             out_shape=(
                 pltpu.VMEM((all_rows, dim), BF16),
                 pltpu.VMEM((piece, dim), F32),
                 pltpu.VMEM((hidden, dim), BF16),
+                pltpu.VMEM((chunk * length, hidden), BF16),
             ),
             in_specs=[pl.BlockSpec(memory_space=pl.ANY)] * 6,
-            out_specs=(vmem, vmem, vmem),
+            out_specs=(vmem,) * 4,
             scratch_shapes=[
                 pltpu.VMEM((all_rows, hidden), BF16),
                 pltpu.VMEM((n_pa, 2, q_count, m_all), jnp.int32),
@@ -426,17 +440,17 @@
             queries, encoder_outputs.reshape(all_rows, hidden), proj_weight,
             bm25_rank[:, 0, :], dense_rank[:, 0, :], custodian,
         )
-        parts = 8 if slots % 8 == 0 else 1
+        parts = 16 if slots % 16 == 0 else 1
         query_grad, hid_grad = pl.pallas_call(
             functools.partial(finish_kernel, parts),
             out_shape=(
                 jax.ShapeDtypeStruct((piece, dim), F32),
                 jax.ShapeDtypeStruct((all_rows, hidden), BF16),
             ),
-            in_specs=[vmem] * 3,
+            in_specs=[vmem] * 4,
             out_specs=(pl.BlockSpec(memory_space=pl.ANY),) * 2,
             scratch_shapes=[pltpu.VMEM((all_rows, hidden), BF16), dma((parts + 1,))],
-        )(*(pltpu.with_memory_space_constraint(x, pltpu.VMEM) for x in (proj_grad, query_part, weight)))
+        )(*(pltpu.with_memory_space_constraint(x, pltpu.VMEM) for x in handed))
         return query_grad, hid_grad.reshape(1, slots, length, hidden)
 
     return jax.shard_map(

time: 26.9 us -> 26.5 us (0.985)
  Pallas kernels: 26 us -> 25.7 us
where the time goes in v4:
time: 26.5 us; the launch traced here: 26.4 us
  Pallas kernels  25.7 us (97%)
  between operations  0.64 us (2%)
    pallas_call x1, Pallas kernels, on_device(): pl.pallas_call(functools.partial(step_kernel, n_pb, n_pa, slots, length,...  23.6 us
    pallas_call x1, Pallas kernels, on_device(): pl.pallas_call(functools.partial(finish_kernel, parts), out_shape=(jax.Sh...  2.16 us

profile of v4, /device:TPU:0, one launch (start us, length us, event | category | flops | bytes accessed | tf_op | source)
XLA Modules:
  0.0 26.4 jit_solution(3296897764752749244)
XLA Ops:
  0.6 23.6 %shard_map.77 = (bf16[2048,128]{1,0:T(8,128)(2,1)S(1)}, f32[64,128]{1,0:T(8,128)S(1)}, bf16[1024,128]{1,0:T(8,128)(2,1)S(1)}, bf16[512,1024]{1,0:T(8,128)(2,1)S(1)}) custom-call(bf16[256,128]{1,0:T(8,128)(2,1)} %q_ref.1, bf16[2048,1024]{1,0:T(8,128)(2,1)} %bitcast.4, bf16[1024,128]{1,0:T(8,128)(2,1)} %w_ref.1, s32[8,64]{1,0:T(8,128)} %bitcast.5, ...), custom_call_target="tpu_custom_call" | custom-call | tf_op jit(solution)/shard_map/pallas_call | solution.py:396
  24.2 2.2 %shard_map.78 = (f32[64,128]{1,0:T(8,128)}, bf16[2048,1024]{1,0:T(8,128)(2,1)}) custom-call(bf16[2048,128]{1,0:T(8,128)(2,1)S(1)} %get-tuple-element.8.pg_ref, f32[64,128]{1,0:T(8,128)S(1)} %get-tuple-element.9.qp_ref, bf16[1024,128]{1,0:T(8,128)(2,1)S(1)} %get-tuple-element.10.w_ref, bf16[512,1024]{1,0:T(8,128)(2,1)S(1)} %get-tuple-element.11.first_ref), custom_call_target="tpu_custom_call" | custom-call | tf_op jit(solution)/shard_map/pallas_call | solution.py:444

commit v5 on v4

--- a/solution.py
+++ b/solution.py
@@ -204,13 +204,15 @@
         lse[pl.ds(k, 1), :] = largest * inv_temp + jnp.log(total)
         inv[pl.ds(k, 1), :] = 1.0 / total
 
+    def set_score(d):
+        parts = [part.astype(F32) for part in three_parts(lse_buf[slot_of(d)])]
+        sums = nn_dot(jnp.concatenate(parts, axis=0).astype(BF16), same_query)
+        first, second, third = (sums[p * slots:(p + 1) * slots] for p in range(3))
+        factor_buf[slot_of(d)] = (first + second + third) * (tau / tokens)
+
     def set_factors(ds):
-        parts = [part.astype(F32) for d in ds for part in three_parts(lse_buf[slot_of(d)])]
-        sums = nn_dot(jnp.concatenate(parts, axis=0).astype(BF16), same_query)
-        for n, d in enumerate(ds):
-            first, second, third = (sums[(3 * n + p) * slots:(3 * n + p + 1) * slots] for p in range(3))
-            score = first + second + third
-            residual = (score * (tau / tokens) - t_exp[d]).astype(BF16).astype(F32)
+        for d in ds:
+            residual = (factor_buf[slot_of(d)] - t_exp[d]).astype(BF16).astype(F32)
             factor_buf[slot_of(d)] = jnp.where(filled, residual * (1.0 / tokens) * inv_buf[slot_of(d)], 0.0)
 
     def spread_targets():
@@ -255,7 +257,9 @@
     def keeps(d):
         return d == 0 or (d > 1 and d % 2 == 1)
 
-    def step(new, old, ready):
+    def step(new, old, ready, scored):
+        if scored is not None:
+            set_score(scored)
         if ready:
             set_factors(ready)
         if old is not None:
@@ -290,7 +294,7 @@
     def finish_pair(d):
         p_copy(d - 1).wait_recv()
         far_out[d // 2] = jnp.transpose(dq_keep[d // 2] + dq_part[d // 2].astype(F32)).astype(BF16)
-        for e in range(n_pa):
+        for e in [n_pa // 2] + [e for e in range(1, n_pa) if e != n_pa // 2] + [0]:
             d_copy(d, e).start()
 
     ready = []
@@ -314,7 +318,7 @@
         if i >= lag:
             first = [d for d in ready if i > lag or d == old]
             ready = [d for d in ready if d not in first]
-        step(new, old, first if i >= lag else [])
+        step(new, old, first if i >= lag else [], new_order[i - 1] if 0 < i <= n_pb else None)
         if i >= lag:
             done.append(old)
             free.append(slot_at[old])

time: 26.5 us -> 26.5 us (level)
  no operation moved by 1% of the time
where the time goes in v5:
time: 26.5 us; the launch traced here: 26.3 us
  Pallas kernels  25.7 us (97%)
  between operations  0.64 us (2%)
    pallas_call x1, Pallas kernels, on_device(): pl.pallas_call(functools.partial(step_kernel, n_pb, n_pa, slots, length,...  23.6 us
    pallas_call x1, Pallas kernels, on_device(): pl.pallas_call(functools.partial(finish_kernel, parts), out_shape=(jax.Sh...  2.16 us

profile of v5, /device:TPU:0, one launch (start us, length us, event | category | flops | bytes accessed | tf_op | source)
XLA Modules:
  0.0 26.3 jit_solution(2501270998902082929)
XLA Ops:
  0.6 23.6 %shard_map.77 = (bf16[2048,128]{1,0:T(8,128)(2,1)S(1)}, f32[64,128]{1,0:T(8,128)S(1)}, bf16[1024,128]{1,0:T(8,128)(2,1)S(1)}, bf16[512,1024]{1,0:T(8,128)(2,1)S(1)}) custom-call(bf16[256,128]{1,0:T(8,128)(2,1)} %q_ref.1, bf16[2048,1024]{1,0:T(8,128)(2,1)} %bitcast.4, bf16[1024,128]{1,0:T(8,128)(2,1)} %w_ref.1, s32[8,64]{1,0:T(8,128)} %bitcast.5, ...), custom_call_target="tpu_custom_call" | custom-call | tf_op jit(solution)/shard_map/pallas_call | solution.py:400
  24.2 2.2 %shard_map.78 = (f32[64,128]{1,0:T(8,128)}, bf16[2048,1024]{1,0:T(8,128)(2,1)}) custom-call(bf16[2048,128]{1,0:T(8,128)(2,1)S(1)} %get-tuple-element.8.pg_ref, f32[64,128]{1,0:T(8,128)S(1)} %get-tuple-element.9.qp_ref, bf16[1024,128]{1,0:T(8,128)(2,1)S(1)} %get-tuple-element.10.w_ref, bf16[512,1024]{1,0:T(8,128)(2,1)S(1)} %get-tuple-element.11.first_ref), custom_call_target="tpu_custom_call" | custom-call | tf_op jit(solution)/shard_map/pallas_call | solution.py:448
